TPU v7x, 512 devices: a whole 4x4x16 slice. The times are simulated.
512 devices in a mesh: rep: 4 (over y), own: 128 (over x, z, core).
Axes of the slice: x: 4, y: 4, z: 16, core: 2. Of those that a mesh axis runs over, the one named last changes fastest.
Arguments:
- local_weights: bfloat16 [4, 192, 384, 768], P('rep', None, 'own'), may hold values from -6 to 6
- anchor: float32 [256, 384, 768], P('own', 'rep'), may hold values from -6 to 6
- momentum: float32 [256, 384, 768], P('own', 'rep'), may hold values from -6 to 6
- owners: int32 [192], replicated, may hold values from 0 to 127, as said below
Outputs:
- new_weights: float32 [192, 384, 768], P(None, 'own')
- new_momentum: float32 [256, 384, 768], P('own', 'rep')
Inputs may be any that keep to these rules, and one draw needn't show every extreme that they name: Blocks 2i and 2i+1 for i < 48 form one attention projection and have the same owner; different projections have different owners; the 96 embedding blocks that follow go to the owners holding no projection, in runs of consecutive blocks; every owner holds at least one block and at most 2, and some owner holds exactly 2.
All inputs are finite; a program needn't handle non-finite values.
Results may differ from a plain program's by a relative error of at most 0.0003.
Values may be sent and summed in bfloat16 or wider, within the bound.
A program may use at most 64 MiB of HBM per device.

v0:
```python
import jax
import jax.numpy as jnp
from jax import lax
from jax.sharding import PartitionSpec as P

outer_rate = 0.7
momentum_rate = 0.9


def local(local_weights, anchor, momentum, owners):
    n_own = lax.axis_size("own")
    n_rep = lax.axis_size("rep")
    blocks = owners.shape[0]
    stripe = local_weights.shape[2]
    width = local_weights.shape[3]
    slots = anchor.shape[0]
    block_rows = stripe * n_own
    index = jnp.arange(blocks, dtype=jnp.int32)
    same = (owners[None, :] == owners[:, None]) & (index[None, :] < index[:, None])
    slot = jnp.sum(same.astype(jnp.int32), axis=1)
    place = owners * slots + slot
    targets = jnp.arange(n_own * slots, dtype=jnp.int32)
    picker = targets[:, None] == place[None, :]
    source = jnp.sum(jnp.where(picker, index[None, :], 0), axis=1)
    valid = jnp.any(picker, axis=1)
    mine = lax.axis_index("own") * slots + jnp.arange(slots, dtype=jnp.int32)
    live = jnp.any(mine[:, None] == place[None, :], axis=1)
    rows_here = local_weights[0]
    flat = rows_here.reshape(blocks, stripe * width)
    outgoing = jnp.where(
        valid[:, None], jnp.take(flat, source, axis=0), jnp.zeros((), jnp.bfloat16)
    )
    outgoing = outgoing.reshape(n_own, slots, stripe, width)
    arrived = lax.all_to_all(outgoing, "own", split_axis=0, concat_axis=2, tiled=True)
    arrived = arrived.reshape(slots, block_rows, width).astype(jnp.float32)
    total = lax.psum_scatter(arrived, "rep", scatter_dimension=1, tiled=True)
    mean_local = total / n_rep
    outer_grad = anchor - mean_local
    moment = momentum_rate * momentum + outer_grad
    updated = anchor - outer_rate * (outer_grad + momentum_rate * moment)
    alive = live[:, None, None]
    new_momentum = jnp.where(alive, moment, 0.0)
    updated = jnp.where(alive, updated, 0.0)
    whole = lax.all_gather(updated, "rep", axis=1, tiled=True)
    whole = whole.reshape(slots, n_own, stripe, width)
    returned = lax.all_to_all(whole, "own", split_axis=1, concat_axis=0, tiled=True)
    returned = returned.reshape(n_own * slots, stripe * width)
    new_weights = jnp.take(returned, place, axis=0)
    new_weights = new_weights.reshape(blocks, stripe, width)
    return (new_weights, new_momentum)


def solution(mesh):
    return jax.shard_map(
        local,
        mesh=mesh,
        in_specs=(P("rep", None, "own", None), P("own", "rep", None), P("own", "rep", None), P()),
        out_specs=(P(None, "own", None), P("own", "rep", None)),
        check_vma=False,
    )
```

profile of v0, /device:TPU:1, one launch (start us, length us, event | category | flops | bytes accessed | tf_op | source)
XLA Modules:
  0.0 356.4 jit_solution(2367220810949827903)
XLA Ops:
  7.2 0.0 all-reduce.3.cloned.1.call-start
  7.2 0.9 convert_reduce_fusion
  8.1 0.7 compare_and_fusion.1
  8.8 0.1 select_reduce_fusion
  8.9 0.1 fusion.2
  9.1 0.1 reduce_sum.24
  9.2 1.9 copy.26
  11.2 0.1 copy.34
  11.3 1.4 gather_fusion
  12.7 0.6 gather.13
  13.3 0.2 broadcast_in_dim.77
  13.5 1.3 select_select_fusion
  14.8 1.0 copy.27
  15.8 79.9 %all_to_all.24 = bf16[128,2,3,768]{3,1,2,0:T(2,128)(2,1)S(1)} all-to-all(bf16[128,2,3,768]{3,1,2,0:T(2,128)(2,1)S(1)} %copy.27), channel_id=1, replica_groups=mesh['rep'=4,'own'=128] {'own'}, dimensions={0} | all-to-all | bytes 2359296 | tf_op jit(solution)/shard_map/all_to_all | solution.py:34
  95.8 2.2 bitcast_convert_fusion
  98.0 0.0 copy-start
  98.0 0.0 copy-start.1
  98.0 0.0 all-reduce.3.cloned.1.call-update
  98.0 0.0 all-gather.2.cloned.1.call-start
  98.0 1.3 dynamic-slice
  100.1 0.2 compare_reduce_fusion
  100.2 69.7 %all-reduce.3.cloned.1.call-done = f32[2,384,768]{2,0,1:T(2,128)} async-done(((f32[2,384,768]{2,0,1:T(2,128)}), f32[2,384,768]{2,0,1:T(2,128)}) %all-reduce.3.cloned.1.call-update) | async-done | bytes 2359312
  170.0 0.0 copy-done
  170.0 0.0 copy-done.1
  170.0 3.3 broadcast_select_fusion.1
  173.3 0.0 all-gather.2.cloned.1.call-update
  173.3 40.7 %all-gather.2.cloned.1.call-done = f32[2,384,768]{2,0,1:T(2,128)} async-done(((f32[2,96,768]{2,0,1:T(2,128)}), f32[2,384,768]{2,0,1:T(2,128)}) %all-gather.2.cloned.1.call-update) | async-done | bytes 2359312 | tf_op jit(solution)/shard_map/all_gather | solution.py:44
  214.0 16.8 %all-to-all-start.1 = ((f32[2,128,3,768]{3,0,2,1:T(2,128)}), f32[2,128,3,768]{3,0,2,1:T(2,128)S(1)}, u32[]{:S(2)}, u32[]{:S(2)}) async-start(f32[2,128,3,768]{3,0,2,1:T(2,128)} %bitcast.26), calls=%async_computation.1 | async-start | bytes 4718592 | tf_op jit(solution)/shard_map/all_to_all | solution.py:46
  230.8 0.9 copy.33
  231.7 109.2 %all-to-all-done.1 = f32[2,128,3,768]{3,0,2,1:T(2,128)S(1)} async-done(((f32[2,128,3,768]{3,0,2,1:T(2,128)}), f32[2,128,3,768]{3,0,2,1:T(2,128)S(1)}, u32[]{:S(2)}, u32[]{:S(2)}) %all-to-all-start.1) | async-done | bytes 2359328 | tf_op jit(solution)/shard_map/all_to_all | solution.py:46
  340.9 0.8 copy.31
  341.7 0.4 copy.35
  342.1 2.5 gather_fusion.1
  344.6 2.8 gather.15
  347.4 0.6 broadcast_select_fusion
  348.0 1.5 copy.32
  (6 shorter events, 0.1 us)
Async XLA Ops:
  7.2 162.8 %all-reduce.3.cloned.1.call-start = ((), (), s32[]{:S(2)}) async-start(), calls=%async_computation.3 | async-start | bytes 4718592
  98.0 72.0 %copy-start = (f32[2,96,768]{2,1,0:T(8,128)S(1)}, f32[2,96,768]{2,1,0:T(8,128)}, u32[]{:S(2)}) copy-start(f32[2,96,768]{2,1,0:T(8,128)} %param.6) | copy-start | bytes 1769476
  98.0 72.0 %copy-start.1 = (f32[2,96,768]{2,1,0:T(8,128)S(1)}, f32[2,96,768]{2,1,0:T(8,128)}, u32[]{:S(2)}) copy-start(f32[2,96,768]{2,1,0:T(8,128)} %param.5) | copy-start | bytes 1769476
  98.0 116.0 %all-gather.2.cloned.1.call-start = ((), (), s32[]{:S(2)}) async-start(), calls=%async_computation.2 | async-start | bytes 2949120 | tf_op jit(solution)/shard_map/all_gather | solution.py:44
  214.0 126.9 %all-to-all-start.1 = ((f32[2,128,3,768]{3,0,2,1:T(2,128)}), f32[2,128,3,768]{3,0,2,1:T(2,128)S(1)}, u32[]{:S(2)}, u32[]{:S(2)}) async-start(f32[2,128,3,768]{3,0,2,1:T(2,128)} %bitcast.26), calls=%async_computation.1 | async-start | bytes 4718592 | tf_op jit(solution)/shard_map/all_to_all | solution.py:46
Sparse Core Ops, SparseCore 0:
  98.1 71.8 all-reduce.2
  173.5 40.4 all-gather.1
where the time goes:
time: 357 us; the launch traced here: 356 us
  waiting for transfers between devices  220 us (62%)
  blocking collectives  79.9 us (22%)
  starting transfers between devices  16.9 us (5%)
  local copies, waits for them, and re-layouts  15.6 us (4%)
  between operations  14.8 us (4%)
  other arithmetic  9.54 us (3%)
    all_to_all x1, waiting for transfers between devices, local(): lax.all_to_all(whole, 'own', split_axis=1, concat_axis=0, tiled=True)  109 us
    all_to_all x1, blocking collectives, local(): lax.all_to_all(outgoing, 'own', split_axis=0, concat_axis=2, tiled=True)  79.9 us
    unnamed x3, waiting for transfers between devices  69.8 us
    all_gather x1, waiting for transfers between devices, local(): whole = lax.all_gather(updated, 'rep', axis=1, tiled=True)  40.7 us
    all_to_all x1, starting transfers between devices, local(): lax.all_to_all(whole, 'own', split_axis=1, concat_axis=0, tiled=True)  16.8 us
  transfers between devices with their start and end apart: 3, of which 3 were waited for; matrix products, arithmetic and copies ran while one was open for 1% of the time, Pallas kernels for 0%

commit v1 on v0

v1 whole, which is shorter than its diff:
```python
import functools
import math

import jax
import jax.numpy as jnp
from jax import lax
from jax.experimental import pallas as pl
from jax.experimental.pallas import tpu as pltpu
from jax.sharding import PartitionSpec as P

MESH = pl.DeviceIdType.MESH

outer_rate = 0.7
momentum_rate = 0.9
MEAN = outer_rate * (1.0 + momentum_rate)
ANCHOR = 1.0 - MEAN
MOMENT = -outer_rate * momentum_rate * momentum_rate

CURVE = 65536.0
LIMIT = 6.0
BOUND_A = 1.01 * LIMIT * (abs(ANCHOR) + abs(MOMENT))
BOUND_N = 1.01 * LIMIT * (abs(ANCHOR) + abs(MOMENT) + MEAN)
BOUND_D = 1.01 * (LIMIT + BOUND_A / abs(ANCHOR))


def _rate(bound):
    return 32767.0 / math.log(1.0 + CURVE * bound)


def encode(value, bound):
    size = jnp.log(1.0 + CURVE * jnp.abs(value)) * _rate(bound)
    code = (size + 0.5).astype(jnp.int32)
    return jnp.where(value < 0, -code, code)


def decode(code, bound):
    size = jnp.abs(code.astype(jnp.float32))
    value = (jnp.exp(size * (1.0 / _rate(bound))) - 1.0) * (1.0 / CURVE)
    return jnp.where(code < 0, -value, value)


def pack(first, second):
    return (second << 16) | (first & 0xFFFF)


def unpack(pair):
    return (pair << 16) >> 16, pair >> 16


def kernel(
    n_rep, n_p, stripe, width, blocks,
    owners_ref, w_hbm, a_hbm, m_hbm, nw_hbm, nm_hbm,
    w_v, a_v, m_v, nm_v, one_hot, picker, sorted_w, f1_in, a_out, a_in, d_out, d_in, table, out_v,
    load_sem, store_sem, f1_send, f1_recv, a_send, a_recv, d_send, d_recv, n_send, n_recv,
):
    lanes = width // 128
    group = 2 * n_p
    y = lax.axis_index("rep")
    own = lax.axis_index("own")
    x, p = own // n_p, own % n_p
    mine = (2 * x - y + 2 * n_rep) % n_rep
    d_x, d_y = mine, x
    a_x, a_y = y, (2 * y - x + 2 * n_rep) % n_rep
    stays = x == y

    barrier = pltpu.get_barrier_semaphore()

    def greet(i, carry):
        q = (p + i) % n_p

        @pl.when(jnp.logical_not(stays & (i == 0)))
        def _():
            pl.semaphore_signal(barrier, inc=1, device_id=(d_y, d_x * n_p + q), device_id_type=MESH)
            pl.semaphore_signal(barrier, inc=1, device_id=(a_y, a_x * n_p + q), device_id_type=MESH)

        return carry

    lax.fori_loop(0, n_p, greet, 0)
    for step in range(1, n_rep):
        pl.semaphore_signal(barrier, inc=1, device_id=((y + step) % n_rep, own), device_id_type=MESH)

    loads = [pltpu.make_async_copy(w_hbm, w_v, load_sem.at[0])]
    for j in range(lanes):
        columns = pl.ds(128 * j, 128)
        loads.append(pltpu.make_async_copy(a_hbm.at[:, :, columns], a_v.at[j], load_sem.at[1 + j]))
        loads.append(pltpu.make_async_copy(m_hbm.at[:, :, columns], m_v.at[j], load_sem.at[1 + lanes + j]))
    for load in loads:
        load.start()

    row = jnp.broadcast_to(owners_ref[...], (blocks, blocks)).astype(jnp.float32)
    first = lax.broadcasted_iota(jnp.int32, (blocks, blocks), 0)
    second = lax.broadcasted_iota(jnp.int32, (blocks, blocks), 1)
    column = jnp.sum(jnp.where(first == second, row, 0.0), axis=1, keepdims=True)
    same = jnp.where(row == column, 1.0, 0.0)
    slot_row = jnp.sum(jnp.where(first < second, same, 0.0), axis=0, keepdims=True)
    slot_column = jnp.sum(jnp.where(second < first, same, 0.0), axis=1, keepdims=True)
    place_row = 2.0 * row[:1] + slot_row
    place_column = 2.0 * column + slot_column
    slots = n_rep * group
    j = lax.broadcasted_iota(jnp.int32, (slots, blocks), 0)
    target = 2 * (j // group * n_p + j % n_p) + j % group // n_p
    one_hot[...] = jnp.where(place_row == target.astype(jnp.float32), 1.0, 0.0).astype(jnp.bfloat16)
    j = lax.broadcasted_iota(jnp.int32, (blocks, slots), 1)
    target = 2 * (j % (n_rep * n_p)) + j // (n_rep * n_p)
    picker[...] = jnp.where(place_column == target.astype(jnp.float32), 1.0, 0.0).astype(jnp.bfloat16)
    alive = []
    for s in range(2):
        here = (2 * own + s).astype(jnp.float32)
        alive.append(jnp.max(jnp.where(place_row == here, 1.0, 0.0), axis=1, keepdims=True) > 0.5)

    for load in loads[1:]:
        load.wait()
    for k in range(stripe):
        for j in range(lanes):
            codes = []
            for s in range(2):
                rows = (j, s, pl.ds(k, n_p, stride=stripe), slice(None))
                codes.append(encode(ANCHOR * a_v[rows] + MOMENT * m_v[rows], BOUND_A))
            a_out[:, pl.ds(k * width + 128 * j, 128)] = pack(*codes)

    loads[0].wait()
    for k in range(stripe):
        moved = jnp.dot(one_hot[...], w_v[k], preferred_element_type=jnp.float32)
        sorted_w[:, k] = moved.astype(jnp.bfloat16).reshape(n_rep, group, width)

    pl.semaphore_wait(barrier, n_rep - 1 + 2 * jnp.where(stays, n_p - 1, n_p))

    def to_rep(source, target_of, send, recv, step, tag):
        return pltpu.make_async_remote_copy(
            src_ref=source, dst_ref=target_of, send_sem=send.at[step - 1], recv_sem=recv.at[tag],
            device_id=((y + step) % n_rep, own), device_id_type=MESH,
        )

    f1 = []
    for step in range(1, n_rep):
        theirs = (2 * x - (y + step) + 2 * n_rep) % n_rep
        f1.append(to_rep(sorted_w.at[theirs], f1_in.at[step - 1], f1_send, f1_recv, step, step - 1))
        f1[-1].start()

    def row_copy(source, target, send, recv, to_y, to_x, q):
        return pltpu.make_async_remote_copy(
            src_ref=source.at[pl.ds(q, 1)], dst_ref=target.at[pl.ds(p, 1)], send_sem=send.at[q], recv_sem=recv.at[p],
            device_id=(to_y, to_x * n_p + q), device_id_type=MESH,
        )

    def own_row(source, target, recv):
        return pltpu.make_async_copy(source.at[pl.ds(p, 1)], target.at[pl.ds(p, 1)], recv.at[p])

    def spread(source, target, send, recv, to_y, to_x):
        def one(i, carry):
            q = (p + i) % n_p
            local = stays & (i == 0)

            @pl.when(local)
            def _():
                own_row(source, target, recv).start()

            @pl.when(jnp.logical_not(local))
            def _():
                row_copy(source, target, send, recv, to_y, to_x, q).start()

            return carry

        lax.fori_loop(0, n_p, one, 0)

    def collect(target, recv):
        def one(q, carry):
            pltpu.make_async_copy(target.at[pl.ds(q, 1)], target.at[pl.ds(q, 1)], recv.at[q]).wait()
            return carry

        lax.fori_loop(0, n_p, one, 0)

    def settle(source, target, send, recv, to_y, to_x):
        def one(i, carry):
            q = (p + i) % n_p

            @pl.when(jnp.logical_not(stays & (i == 0)))
            def _():
                row_copy(source, target, send, recv, to_y, to_x, q).wait_send()

            return carry

        lax.fori_loop(0, n_p, one, 0)

    spread(a_out, a_in, a_send, a_recv, a_y, a_x)

    for copy in f1:
        copy.wait_recv()
    collect(a_in, a_recv)
    for k in range(stripe):
        for j in range(0, width, 256):
            columns = pl.ds(j, 256)
            total = sorted_w[mine, k, :, columns].astype(jnp.float32)
            for step in range(1, n_rep):
                total += f1_in[step - 1, k, :, columns].astype(jnp.float32)
            mean = total * (1.0 / n_rep)
            shares = unpack(a_in[:, pl.ds(k * width + j, 256)])
            new_codes, mean_codes = [], []
            for s in range(2):
                share = decode(shares[s], BOUND_A)
                here = mean[s * n_p : (s + 1) * n_p]
                new_codes.append(encode(share + MEAN * here, BOUND_N))
                mean_codes.append(encode(here - (1.0 / ANCHOR) * share, BOUND_D))
            table[mine, k, :, columns] = pack(*new_codes)
            d_out[:, pl.ds(k * width + j, 256)] = pack(*mean_codes)

    spread(d_out, d_in, d_send, d_recv, d_y, d_x)
    gather = []
    for step in range(1, n_rep):
        gather.append(to_rep(table.at[mine], table.at[mine], n_send, n_recv, step, step - 1))
        gather[-1].start()

    collect(d_in, d_recv)
    for k in range(stripe):
        for j in range(lanes):
            columns = pl.ds(k * width + 128 * j, 128)
            shares, gaps = unpack(a_out[:, columns]), unpack(d_in[:, columns])
            for s in range(2):
                rows = (j, s, pl.ds(k, n_p, stride=stripe), slice(None))
                mean = decode(gaps[s], BOUND_D) + (1.0 / ANCHOR) * decode(shares[s], BOUND_A)
                moment = momentum_rate * m_v[rows] + (a_v[rows] - mean)
                nm_v[rows] = jnp.where(alive[s], moment, 0.0)
    stores = []
    for j in range(lanes):
        stores.append(pltpu.make_async_copy(nm_v.at[j], nm_hbm.at[:, :, pl.ds(128 * j, 128)], store_sem.at[j]))
        stores[-1].start()

    for copy in gather:
        copy.wait_recv()
    for k in range(stripe):
        pairs = table[:, k].reshape(n_rep * n_p, width)
        low = jnp.concatenate([pairs & 255, (pairs >> 16) & 255], axis=0)
        high = jnp.concatenate([(pairs >> 8) & 255, pairs >> 24], axis=0)
        picked = []
        for part in (low, high):
            part = part.astype(jnp.float32).astype(jnp.bfloat16)
            picked.append(jnp.dot(picker[...], part, preferred_element_type=jnp.float32))
        code = picked[0] + 256.0 * picked[1]
        code = jnp.where(code >= 32768.0, code - 65536.0, code)
        out_v[k] = decode(code, BOUND_N)
        stores.append(pltpu.make_async_copy(out_v.at[k], nw_hbm.at[k], store_sem.at[lanes + k]))
        stores[-1].start()

    for copy in f1 + gather:
        copy.wait_send()
    settle(a_out, a_in, a_send, a_recv, a_y, a_x)
    settle(d_out, d_in, d_send, d_recv, d_y, d_x)
    for store in stores:
        store.wait()


def local(local_weights, anchor, momentum, owners):
    n_rep = lax.axis_size("rep")
    n_p = lax.axis_size("own") // n_rep
    blocks = owners.shape[0]
    stripe, width = local_weights.shape[2:]
    lanes = width // 128
    group = 2 * n_p
    rows = jnp.transpose(local_weights[0], (1, 0, 2))
    tall = (lanes, *anchor.shape[:2], 128)
    pairs = (n_p, stripe * width)
    vmem, dma = pltpu.VMEM, pltpu.SemaphoreType.DMA
    new_weights, new_momentum = pl.pallas_call(
        functools.partial(kernel, n_rep, n_p, stripe, width, blocks),
        out_shape=(
            jax.ShapeDtypeStruct(rows.shape, jnp.float32),
            jax.ShapeDtypeStruct(momentum.shape, jnp.float32),
        ),
        in_specs=[pl.BlockSpec(memory_space=pltpu.VMEM)] + [pl.BlockSpec(memory_space=pl.ANY)] * 3,
        out_specs=(pl.BlockSpec(memory_space=pl.ANY),) * 2,
        scratch_shapes=[
            vmem(rows.shape, jnp.bfloat16),
            vmem(tall, jnp.float32),
            vmem(tall, jnp.float32),
            vmem(tall, jnp.float32),
            vmem((n_rep * group, blocks), jnp.bfloat16),
            vmem((blocks, n_rep * group), jnp.bfloat16),
            vmem((n_rep, stripe, group, width), jnp.bfloat16),
            vmem((n_rep - 1, stripe, group, width), jnp.bfloat16),
            vmem(pairs, jnp.int32),
            vmem(pairs, jnp.int32),
            vmem(pairs, jnp.int32),
            vmem(pairs, jnp.int32),
            vmem((n_rep, stripe, n_p, width), jnp.int32),
            vmem(rows.shape, jnp.float32),
            dma((1 + 2 * lanes,)),
            dma((lanes + stripe,)),
            dma((n_rep - 1,)),
            dma((n_rep - 1,)),
            dma((n_p,)),
            dma((n_p,)),
            dma((n_p,)),
            dma((n_p,)),
            dma((n_rep - 1,)),
            dma((n_rep - 1,)),
        ],
        compiler_params=pltpu.CompilerParams(collective_id=0, has_side_effects=True, vmem_limit_bytes=48 << 20),
    )(owners.reshape(1, blocks), rows, anchor, momentum)
    return jnp.transpose(new_weights, (1, 0, 2)), new_momentum


def solution(mesh):
    return jax.shard_map(
        local,
        mesh=mesh,
        in_specs=(P("rep", None, "own", None), P("own", "rep", None), P("own", "rep", None), P()),
        out_specs=(P(None, "own", None), P("own", "rep", None)),
        check_vma=False,
    )
```

time: 357 us -> 76.3 us (0.21)
  waiting for transfers between devices: 220 us -> 0 us
  blocking collectives: 79.9 us -> 0 us
  Pallas kernels: 0 us -> 69.4 us
  starting transfers between devices: 16.9 us -> 0 us
  between operations: 14.8 us -> 0.65 us
  local copies, waits for them, and re-layouts: 15.6 us -> 5.99 us
  other arithmetic: 9.54 us -> 0 us
    all_to_all x1 -> x0, waiting for transfers between devices: 109 us -> none  [local(): lax.all_to_all(whole, 'own', split_axis=1, concat_axis=0, tiled=True)]
    all_to_all x1 -> x0, blocking collectives: 79.9 us -> none  [local(): lax.all_to_all(outgoing, 'own', split_axis=0, concat_axis=2, tiled=True)]
    unnamed x3 -> x0, waiting for transfers between devices: 69.8 us -> none
    pallas_call x0 -> x1, Pallas kernels: none -> 69.4 us  [local(): pl.pallas_call(functools.partial(kernel, n_rep, n_p, stripe, width, block...]
    all_gather x1 -> x0, waiting for transfers between devices: 40.7 us -> none  [local(): whole = lax.all_gather(updated, 'rep', axis=1, tiled=True)]
    all_to_all x1 -> x0, starting transfers between devices: 16.8 us -> none  [local(): lax.all_to_all(whole, 'own', split_axis=1, concat_axis=0, tiled=True)]
    gather x4 -> x0, local copies, waits for them, and re-layouts: 7.26 us -> none  [the longest x2 5.29 us: local(): new_weights = jnp.take(returned, place, axis=0)]
    select_n x5 -> x0, other arithmetic: 5.26 us -> none  [the longest x1 3.33 us: local(): new_momentum = jnp.where(alive, moment, 0.0)]
  transfers between devices with their start and end apart: 3 -> 0, of which waited for: 3 -> 0; matrix products, arithmetic and copies ran while one was open for 1% -> 0% of each run, Pallas kernels for 0% -> 0%
where the time goes in v1:
time: 76.3 us; the launch traced here: 76 us
  Pallas kernels  69.4 us (91%)
  local copies, waits for them, and re-layouts  5.99 us (8%)
    pallas_call x1, Pallas kernels, local(): pl.pallas_call(functools.partial(kernel, n_rep, n_p, stripe, width, block...  69.4 us
    unnamed x10, local copies, waits for them, and re-layouts  5.99 us

profile of v1, /device:TPU:1, one launch (start us, length us, event | category | flops | bytes accessed | tf_op | source)
XLA Modules:
  0.0 76.0 jit_solution(8814553593217559586)
XLA Ops:
  0.6 0.0 copy-start
  0.6 1.2 %copy-done = bf16[1,192,3,768]{3,1,2,0:T(8,128)(2,1)S(1)} copy-done((bf16[1,192,3,768]{3,1,2,0:T(8,128)(2,1)S(1)}, bf16[1,192,3,768]{3,1,2,0:T(8,128)(2,1)}, u32[]{:S(2)}) %copy-start) | copy-done | bytes 884760
  1.8 0.0 copy-start.1
  1.8 1.1 %copy-done.1 = f32[2,96,768]{2,1,0:T(8,128)S(1)} copy-done((f32[2,96,768]{2,1,0:T(8,128)S(1)}, f32[2,96,768]{2,1,0:T(8,128)}, u32[]{:S(2)}) %copy-start.1) | copy-done | bytes 589848
  2.9 0.0 copy-start.2
  2.9 1.1 %copy-done.2 = f32[2,96,768]{2,1,0:T(8,128)S(1)} copy-done((f32[2,96,768]{2,1,0:T(8,128)S(1)}, f32[2,96,768]{2,1,0:T(8,128)}, u32[]{:S(2)}) %copy-start.2) | copy-done | bytes 589848
  3.9 0.0 copy-start.3
  3.9 0.7 copy-done.3
  4.6 69.4 %shard_map.59 = (f32[3,192,768]{2,1,0:T(8,128)S(1)}, f32[2,96,768]{2,1,0:T(8,128)S(1)}) custom-call(s32[1,192]{1,0:T(1,128)S(1)} %bitcast.7, bf16[3,192,768]{2,1,0:T(8,128)(2,1)S(1)} %bitcast.6, f32[2,96,768]{2,1,0:T(8,128)S(1)} %copy-done.1, f32[2,96,768]{2,1,0:T(8,128)S(1)} %copy-done.2), custom_call_target="tpu_custom_call" | custom-call | tf_op jit(solution)/shard_map/pallas_call | solution.py:263
  74.0 1.2 %copy.8 = f32[192,3,768]{2,0,1:T(8,128)} copy(f32[192,3,768]{2,0,1:T(8,128)S(1)} %bitcast.5) | data formatting | bytes 3538944
  75.2 0.8 %copy.9 = f32[2,96,768]{2,1,0:T(8,128)} copy(f32[2,96,768]{2,1,0:T(8,128)S(1)} %get-tuple-element.9) | data formatting | bytes 1179648
Async XLA Ops:
  0.6 1.2 %copy-start = (bf16[1,192,3,768]{3,1,2,0:T(8,128)(2,1)S(1)}, bf16[1,192,3,768]{3,1,2,0:T(8,128)(2,1)}, u32[]{:S(2)}) copy-start(bf16[1,192,3,768]{3,1,2,0:T(8,128)(2,1)} %param.4) | copy-start | bytes 2654212
  1.8 1.1 %copy-start.1 = (f32[2,96,768]{2,1,0:T(8,128)S(1)}, f32[2,96,768]{2,1,0:T(8,128)}, u32[]{:S(2)}) copy-start(f32[2,96,768]{2,1,0:T(8,128)} %a_hbm.1) | copy-start | bytes 1769476
  2.9 1.1 %copy-start.2 = (f32[2,96,768]{2,1,0:T(8,128)S(1)}, f32[2,96,768]{2,1,0:T(8,128)}, u32[]{:S(2)}) copy-start(f32[2,96,768]{2,1,0:T(8,128)} %m_hbm.1) | copy-start | bytes 1769476
  3.9 0.7 copy-start.3

commit v2 on v1

v2 whole, which is shorter than its diff:
```python
import functools
import math

import jax
import jax.numpy as jnp
from jax import lax
from jax.experimental import pallas as pl
from jax.experimental.pallas import tpu as pltpu
from jax.sharding import PartitionSpec as P

MESH = pl.DeviceIdType.MESH

outer_rate = 0.7
momentum_rate = 0.9
MEAN = outer_rate * (1.0 + momentum_rate)
ANCHOR = 1.0 - MEAN
MOMENT = -outer_rate * momentum_rate * momentum_rate

CURVE = 65536.0
LIMIT = 6.0
BOUND_A = 1.01 * LIMIT * (abs(ANCHOR) + abs(MOMENT))
BOUND_N = 1.01 * LIMIT * (abs(ANCHOR) + abs(MOMENT) + MEAN)
BOUND_D = 1.01 * (LIMIT + BOUND_A / abs(ANCHOR))


def _rate(bound):
    return 32767.0 / math.log(1.0 + CURVE * bound)


def encode(value, bound):
    size = jnp.log(1.0 + CURVE * jnp.abs(value)) * _rate(bound)
    code = (size + 0.5).astype(jnp.int32)
    return jnp.where(value < 0, -code, code)


def decode(code, bound):
    size = jnp.abs(code.astype(jnp.float32))
    value = (jnp.exp(size * (1.0 / _rate(bound))) - 1.0) * (1.0 / CURVE)
    return jnp.where(code < 0, -value, value)


def pack(first, second):
    return (second << 16) | (first & 0xFFFF)


def unpack(pair):
    return (pair << 16) >> 16, pair >> 16


def kernel(
    n_rep, n_p, stripe, width, blocks,
    owners_hbm, w_hbm, a_hbm, m_hbm, nw_hbm, nm_hbm,
    owners_v, w_v, a_v, m_v, nm_v, one_hot, picker, sorted_w, f1_in, a_out, a_in, d_out, d_in, table, out_v,
    load_sem, store_sem, f1_send, f1_recv, a_send, a_recv, d_send, d_recv, r_send, r_recv, t_send, t_recv,
):
    lanes = width // 128
    group = 2 * n_p
    y = lax.axis_index("rep")
    own = lax.axis_index("own")
    x, p = own // n_p, own % n_p
    diagonal = x == y

    barrier = pltpu.get_barrier_semaphore()

    def hello(to_y, to_own):
        pl.semaphore_signal(barrier, inc=1, device_id=(to_y, to_own), device_id_type=MESH)

    def greet(i, carry):
        hello(y, x * n_p + (p + i) % n_p)
        return carry

    lax.fori_loop(1, n_p, greet, 0)
    for i in range(1, n_rep):
        hello((y + i) % n_rep, own)
        hello(y, (x + i) % n_rep * n_p + p)
    for i in range(n_rep):

        @pl.when(jnp.logical_not(diagonal & (x == i)))
        def _():
            hello(x, i * n_p + p)
            hello(i, y * n_p + p)

    loads = [pltpu.make_async_copy(owners_hbm, owners_v, load_sem.at[0])]
    for j in range(lanes):
        columns = pl.ds(128 * j, 128)
        loads.append(pltpu.make_async_copy(a_hbm.at[:, :, columns], a_v.at[j], load_sem.at[2 + j]))
        loads.append(pltpu.make_async_copy(m_hbm.at[:, :, columns], m_v.at[j], load_sem.at[2 + lanes + j]))
    loads.append(pltpu.make_async_copy(w_hbm, w_v, load_sem.at[1]))
    for load in loads:
        load.start()

    loads[0].wait()
    row = jnp.broadcast_to(owners_v[...], (blocks, blocks)).astype(jnp.float32)
    first = lax.broadcasted_iota(jnp.int32, (blocks, blocks), 0)
    second = lax.broadcasted_iota(jnp.int32, (blocks, blocks), 1)
    column = jnp.sum(jnp.where(first == second, row, 0.0), axis=1, keepdims=True)
    same = jnp.where(row == column, 1.0, 0.0)
    slot_row = jnp.sum(jnp.where(first < second, same, 0.0), axis=0, keepdims=True)
    slot_column = jnp.sum(jnp.where(second < first, same, 0.0), axis=1, keepdims=True)
    place_row = 2.0 * row[:1] + slot_row
    place_column = 2.0 * column + slot_column
    slots = n_rep * group
    j = lax.broadcasted_iota(jnp.int32, (slots, blocks), 0)
    target = 2 * (j // group * n_p + j % n_p) + j % group // n_p
    one_hot[...] = jnp.where(place_row == target.astype(jnp.float32), 1.0, 0.0).astype(jnp.bfloat16)
    j = lax.broadcasted_iota(jnp.int32, (blocks, slots), 1)
    target = 2 * (j % (n_rep * n_p)) + j // (n_rep * n_p)
    picker[...] = jnp.where(place_column == target.astype(jnp.float32), 1.0, 0.0).astype(jnp.bfloat16)
    alive = []
    for s in range(2):
        here = (2 * own + s).astype(jnp.float32)
        alive.append(jnp.max(jnp.where(place_row == here, 1.0, 0.0), axis=1, keepdims=True) > 0.5)

    for load in loads[1:]:
        load.wait()
    for k in range(stripe):
        for j in range(lanes):
            codes = []
            for s in range(2):
                rows = (j, s, pl.ds(k, n_p, stride=stripe), slice(None))
                codes.append(encode(ANCHOR * a_v[rows] + MOMENT * m_v[rows], BOUND_A))
            a_out[k, :, pl.ds(128 * j, 128)] = pack(*codes)

    for k in range(stripe):
        moved = jnp.dot(one_hot[...], w_v[k], preferred_element_type=jnp.float32)
        sorted_w[:, k] = moved.astype(jnp.bfloat16).reshape(n_rep, group, width)

    pl.semaphore_wait(barrier, n_p - 1 + 2 * (n_rep - 1) + 2 * jnp.where(diagonal, n_rep - 1, n_rep))

    def row_copy(source, target, send, recv, k, q):
        return pltpu.make_async_remote_copy(
            src_ref=source.at[k, pl.ds(q, 1)], dst_ref=target.at[k, pl.ds(p, 1)],
            send_sem=send.at[k, q], recv_sem=recv.at[k, p], device_id=(y, x * n_p + q), device_id_type=MESH,
        )

    def spread(source, target, send, recv, k):
        rows = pl.ds(p, 1)
        pltpu.make_async_copy(source.at[k, rows], target.at[k, rows], recv.at[k, p]).start()

        def one(i, carry):
            row_copy(source, target, send, recv, k, (p + i) % n_p).start()
            return carry

        lax.fori_loop(1, n_p, one, 0)

    def collect(target, recv, k):
        def one(q, carry):
            rows = target.at[k, pl.ds(q, 1)]
            pltpu.make_async_copy(rows, rows, recv.at[k, q]).wait()
            return carry

        lax.fori_loop(0, n_p, one, 0)

    def settle(source, target, send, recv, k):
        def one(i, carry):
            row_copy(source, target, send, recv, k, (p + i) % n_p).wait_send()
            return carry

        lax.fori_loop(1, n_p, one, 0)

    def f1_copy(k, g):
        return pltpu.make_async_remote_copy(
            src_ref=sorted_w.at[g, k], dst_ref=f1_in.at[y, k], send_sem=f1_send.at[k, g], recv_sem=f1_recv.at[k, y],
            device_id=(x, g * n_p + p), device_id_type=MESH,
        )

    for k in range(stripe):
        for i in range(n_rep):
            g = (x + 1 + i) % n_rep
            stays = diagonal & (g == x)

            @pl.when(stays)
            def _():
                pltpu.make_async_copy(sorted_w.at[g, k], f1_in.at[y, k], f1_recv.at[k, y]).start()

            @pl.when(jnp.logical_not(stays))
            def _():
                f1_copy(k, g).start()

        spread(a_out, a_in, a_send, a_recv, k)

    def spot(plane):
        return jnp.where(plane == x, x, n_rep + plane)

    def pass_on(k, plane):
        return pltpu.make_async_remote_copy(
            src_ref=table.at[n_rep + plane, k], dst_ref=table.at[x, k], send_sem=t_send.at[k, plane],
            recv_sem=t_recv.at[k, x], device_id=(y, plane * n_p + p), device_id_type=MESH,
        )

    def start_pass_on(k, plane):
        @pl.when(plane != x)
        def _():
            pass_on(k, plane).start()

    def r_copy(k, step):
        return pltpu.make_async_remote_copy(
            src_ref=table.at[spot(y), k], dst_ref=table.at[spot(y), k], send_sem=r_send.at[k, step - 1],
            recv_sem=r_recv.at[k, y], device_id=((y + step) % n_rep, own), device_id_type=MESH,
        )

    def relay(k):
        for step in sorted(range(1, n_rep), key=lambda step: min(step, n_rep - step)):
            plane = (y + step) % n_rep
            place = table.at[spot(plane), k]
            pltpu.make_async_copy(place, place, r_recv.at[k, plane]).wait()
            start_pass_on(k, plane)

    for k in range(stripe):
        for i in range(n_rep):
            pltpu.make_async_copy(f1_in.at[i, k], f1_in.at[i, k], f1_recv.at[k, i]).wait()
        collect(a_in, a_recv, k)
        for j in range(0, width, 256):
            columns = pl.ds(j, 256)
            total = f1_in[0, k, :, columns].astype(jnp.float32)
            for i in range(1, n_rep):
                total += f1_in[i, k, :, columns].astype(jnp.float32)
            mean = total * (1.0 / n_rep)
            shares = unpack(a_in[k, :, columns])
            new_codes, mean_codes = [], []
            for s in range(2):
                share = decode(shares[s], BOUND_A)
                here = mean[s * n_p : (s + 1) * n_p]
                new_codes.append(encode(share + MEAN * here, BOUND_N))
                mean_codes.append(encode(here - (1.0 / ANCHOR) * share, BOUND_D))
            table[spot(y), k, :, columns] = pack(*new_codes)
            d_out[k, :, columns] = pack(*mean_codes)
        for step in sorted(range(1, n_rep), key=lambda step: -min(step, n_rep - step)):
            r_copy(k, step).start()
        start_pass_on(k, y)
        spread(d_out, d_in, d_send, d_recv, k)
        if k > 0:
            relay(k - 1)
    relay(stripe - 1)

    for k in range(stripe):
        collect(d_in, d_recv, k)
        for j in range(lanes):
            columns = pl.ds(128 * j, 128)
            shares, gaps = unpack(a_out[k, :, columns]), unpack(d_in[k, :, columns])
            for s in range(2):
                rows = (j, s, pl.ds(k, n_p, stride=stripe), slice(None))
                mean = decode(gaps[s], BOUND_D) + (1.0 / ANCHOR) * decode(shares[s], BOUND_A)
                moment = momentum_rate * m_v[rows] + (a_v[rows] - mean)
                nm_v[rows] = jnp.where(alive[s], moment, 0.0)
    stores = []
    for j in range(lanes):
        stores.append(pltpu.make_async_copy(nm_v.at[j], nm_hbm.at[:, :, pl.ds(128 * j, 128)], store_sem.at[j]))
        stores[-1].start()

    for k in range(stripe):
        for i in range(1, n_rep):
            there = (x + i) % n_rep
            place = table.at[there, k]
            pltpu.make_async_copy(place, place, t_recv.at[k, there]).wait()
        pairs = table[:n_rep, k].reshape(n_rep * n_p, width)
        low = jnp.concatenate([pairs & 255, (pairs >> 16) & 255], axis=0)
        high = jnp.concatenate([(pairs >> 8) & 255, pairs >> 24], axis=0)
        picked = []
        for part in (low, high):
            part = part.astype(jnp.float32).astype(jnp.bfloat16)
            picked.append(jnp.dot(picker[...], part, preferred_element_type=jnp.float32))
        code = picked[0] + 256.0 * picked[1]
        code = jnp.where(code >= 32768.0, code - 65536.0, code)
        out_v[k] = decode(code, BOUND_N)
        stores.append(pltpu.make_async_copy(out_v.at[k], nw_hbm.at[k], store_sem.at[lanes + k]))
        stores[-1].start()

    for k in range(stripe):
        for i in range(n_rep):

            @pl.when(jnp.logical_not(diagonal & (x == i)))
            def _():
                f1_copy(k, i).wait_send()

            @pl.when(x != i)
            def _():
                pass_on(k, i).wait_send()

        for step in range(1, n_rep):
            r_copy(k, step).wait_send()
        settle(a_out, a_in, a_send, a_recv, k)
        settle(d_out, d_in, d_send, d_recv, k)
    for store in stores:
        store.wait()


def local(local_weights, anchor, momentum, owners):
    n_rep = lax.axis_size("rep")
    n_p = lax.axis_size("own") // n_rep
    blocks = owners.shape[0]
    stripe, width = local_weights.shape[2:]
    lanes = width // 128
    group = 2 * n_p
    rows = jnp.transpose(local_weights[0], (1, 0, 2))
    tall = (lanes, *anchor.shape[:2], 128)
    pairs = (stripe, n_p, width)
    vmem, dma = pltpu.VMEM, pltpu.SemaphoreType.DMA
    new_weights, new_momentum = pl.pallas_call(
        functools.partial(kernel, n_rep, n_p, stripe, width, blocks),
        out_shape=(
            jax.ShapeDtypeStruct(rows.shape, jnp.float32),
            jax.ShapeDtypeStruct(momentum.shape, jnp.float32),
        ),
        in_specs=[pl.BlockSpec(memory_space=pl.ANY)] * 4,
        out_specs=(pl.BlockSpec(memory_space=pl.ANY),) * 2,
        scratch_shapes=[
            vmem((1, blocks), jnp.int32),
            vmem(rows.shape, jnp.bfloat16),
            vmem(tall, jnp.float32),
            vmem(tall, jnp.float32),
            vmem(tall, jnp.float32),
            vmem((n_rep * group, blocks), jnp.bfloat16),
            vmem((blocks, n_rep * group), jnp.bfloat16),
            vmem((n_rep, stripe, group, width), jnp.bfloat16),
            vmem((n_rep, stripe, group, width), jnp.bfloat16),
            vmem(pairs, jnp.int32),
            vmem(pairs, jnp.int32),
            vmem(pairs, jnp.int32),
            vmem(pairs, jnp.int32),
            vmem((2 * n_rep, *pairs), jnp.int32),
            vmem(rows.shape, jnp.float32),
            dma((2 + 2 * lanes,)),
            dma((lanes + stripe,)),
            dma((stripe, n_rep)),
            dma((stripe, n_rep)),
            dma((stripe, n_p)),
            dma((stripe, n_p)),
            dma((stripe, n_p)),
            dma((stripe, n_p)),
            dma((stripe, n_rep - 1)),
            dma((stripe, n_rep)),
            dma((stripe, n_rep)),
            dma((stripe, n_rep)),
        ],
        compiler_params=pltpu.CompilerParams(collective_id=0, has_side_effects=True, vmem_limit_bytes=64000000),
    )(owners.reshape(1, blocks), rows, anchor, momentum)
    return jnp.transpose(new_weights, (1, 0, 2)), new_momentum


def solution(mesh):
    return jax.shard_map(
        local,
        mesh=mesh,
        in_specs=(P("rep", None, "own", None), P("own", "rep", None), P("own", "rep", None), P()),
        out_specs=(P(None, "own", None), P("own", "rep", None)),
        check_vma=False,
    )
```

time: 76.3 us -> 63.7 us (0.83)
  the two profiles are of different devices: /device:TPU:1 before, /device:TPU:14 now
where the time goes in v2:
time: 63.7 us; the launch traced here: 63.5 us
  Pallas kernels  59.1 us (93%)
  local copies, waits for them, and re-layouts  3.68 us (6%)
  between operations  0.65 us (1%)
    pallas_call x1, Pallas kernels, local(): pl.pallas_call(functools.partial(kernel, n_rep, n_p, stripe, width, block...  59.1 us
    unnamed x4, local copies, waits for them, and re-layouts  3.68 us

profile of v2, /device:TPU:14, one launch (start us, length us, event | category | flops | bytes accessed | tf_op | source)
XLA Modules:
  0.0 63.5 jit_solution(18018881687935020364)
XLA Ops:
  0.6 59.1 %shard_map.59 = (f32[3,192,768]{2,1,0:T(8,128)}, f32[2,96,768]{2,1,0:T(8,128)}) custom-call(s32[1,192]{1,0:T(1,128)} %bitcast.7, bf16[3,192,768]{2,1,0:T(8,128)(2,1)} %bitcast.6, f32[2,96,768]{2,1,0:T(8,128)} %a_hbm.1, f32[2,96,768]{2,1,0:T(8,128)} %m_hbm.1), custom_call_target="tpu_custom_call" | custom-call | tf_op jit(solution)/shard_map/pallas_call | solution.py:299
  59.8 0.0 copy-start
  59.8 2.9 %copy.8 = f32[192,3,768]{2,0,1:T(8,128)} copy(f32[192,3,768]{2,0,1:T(8,128)} %bitcast.5) | data formatting | bytes 3538944
  62.7 0.0 copy-done
  62.7 0.8 %copy.9 = f32[2,96,768]{2,1,0:T(8,128)} copy(f32[2,96,768]{2,1,0:T(8,128)S(1)} %copy-done) | data formatting | bytes 1179648
Async XLA Ops:
  59.8 2.9 %copy-start = (f32[2,96,768]{2,1,0:T(8,128)S(1)}, f32[2,96,768]{2,1,0:T(8,128)}, u32[]{:S(2)}) copy-start(f32[2,96,768]{2,1,0:T(8,128)} %get-tuple-element.9) | copy-start | bytes 1769476

commit v3 on v2

--- a/solution.py
+++ b/solution.py
@@ -51,7 +51,7 @@
     n_rep, n_p, stripe, width, blocks,
     owners_hbm, w_hbm, a_hbm, m_hbm, nw_hbm, nm_hbm,
     owners_v, w_v, a_v, m_v, nm_v, one_hot, picker, sorted_w, f1_in, a_out, a_in, d_out, d_in, table, out_v,
-    load_sem, store_sem, f1_send, f1_recv, a_send, a_recv, d_send, d_recv, r_send, r_recv, t_send, t_recv,
+    load_sem, store_sem, f1_send, f1_recv, a_send, a_recv, d_send, d_recv, r_send, r_recv, t_send, t_recv, far_sem, near_sem,
 ):
     lanes = width // 128
     group = 2 * n_p
@@ -65,11 +65,19 @@
     def hello(to_y, to_own):
         pl.semaphore_signal(barrier, inc=1, device_id=(to_y, to_own), device_id_type=MESH)
 
-    def greet(i, carry):
-        hello(y, x * n_p + (p + i) % n_p)
-        return carry
-
-    lax.fori_loop(1, n_p, greet, 0)
+    n_z = n_p // 2
+    half = (n_z // 2 + 1) // 2
+    z, core = p // 2, p % 2
+    reach = [step for step in range(1, n_z) if min(step, n_z - step) <= half]
+    jumps = sorted({half, n_z - half})
+    partner = x * n_p + 2 * z + 1 - core
+
+    def ring(step):
+        return x * n_p + 2 * ((z + step) % n_z) + core
+
+    for step in reach:
+        hello(y, ring(step))
+    hello(y, partner)
     for i in range(1, n_rep):
         hello((y + i) % n_rep, own)
         hello(y, (x + i) % n_rep * n_p + p)
@@ -111,7 +119,66 @@
         here = (2 * own + s).astype(jnp.float32)
         alive.append(jnp.max(jnp.where(place_row == here, 1.0, 0.0), axis=1, keepdims=True) > 0.5)
 
-    for load in loads[1:]:
+    loads[-1].wait()
+    for k in range(stripe):
+        moved = jnp.dot(one_hot[...], w_v[k], preferred_element_type=jnp.float32)
+        sorted_w[:, k] = moved.astype(jnp.bfloat16).reshape(n_rep, group, width)
+
+    pl.semaphore_wait(barrier, len(reach) + 1 + 2 * (n_rep - 1) + 2 * jnp.where(diagonal, n_rep - 1, n_rep))
+    for i, step in enumerate(jumps):
+        pl.semaphore_signal(far_sem.at[i], inc=1, device_id=(y, ring(step)), device_id_type=MESH)
+
+    def row_copy(source, target, send, recv, k, q):
+        return pltpu.make_async_remote_copy(
+            src_ref=source.at[k, pl.ds(q, 1)], dst_ref=target.at[k, pl.ds(p, 1)],
+            send_sem=send.at[k, q], recv_sem=recv.at[k, p], device_id=(y, x * n_p + q), device_id_type=MESH,
+        )
+
+    def spread(source, target, send, recv, k):
+        rows = pl.ds(p, 1)
+        pltpu.make_async_copy(source.at[k, rows], target.at[k, rows], recv.at[k, p]).start()
+
+        def one(i, carry):
+            row_copy(source, target, send, recv, k, (p + i) % n_p).start()
+            return carry
+
+        lax.fori_loop(1, n_p, one, 0)
+
+    def collect(target, recv, k):
+        def one(q, carry):
+            rows = target.at[k, pl.ds(q, 1)]
+            pltpu.make_async_copy(rows, rows, recv.at[k, q]).wait()
+            return carry
+
+        lax.fori_loop(0, n_p, one, 0)
+
+    def settle(source, target, send, recv, k):
+        def one(i, carry):
+            row_copy(source, target, send, recv, k, (p + i) % n_p).wait_send()
+            return carry
+
+        lax.fori_loop(1, n_p, one, 0)
+
+    def f1_copy(k, g):
+        return pltpu.make_async_remote_copy(
+            src_ref=sorted_w.at[g, k], dst_ref=f1_in.at[y, k], send_sem=f1_send.at[k, g], recv_sem=f1_recv.at[k, y],
+            device_id=(x, g * n_p + p), device_id_type=MESH,
+        )
+
+    for k in range(stripe):
+        for i in range(n_rep):
+            g = (x + 1 + i) % n_rep
+            stays = diagonal & (g == x)
+
+            @pl.when(stays)
+            def _():
+                pltpu.make_async_copy(sorted_w.at[g, k], f1_in.at[y, k], f1_recv.at[k, y]).start()
+
+            @pl.when(jnp.logical_not(stays))
+            def _():
+                f1_copy(k, g).start()
+
+    for load in loads[1:-1]:
         load.wait()
     for k in range(stripe):
         for j in range(lanes):
@@ -121,62 +188,11 @@
                 codes.append(encode(ANCHOR * a_v[rows] + MOMENT * m_v[rows], BOUND_A))
             a_out[k, :, pl.ds(128 * j, 128)] = pack(*codes)
 
-    for k in range(stripe):
-        moved = jnp.dot(one_hot[...], w_v[k], preferred_element_type=jnp.float32)
-        sorted_w[:, k] = moved.astype(jnp.bfloat16).reshape(n_rep, group, width)
-
-    pl.semaphore_wait(barrier, n_p - 1 + 2 * (n_rep - 1) + 2 * jnp.where(diagonal, n_rep - 1, n_rep))
-
-    def row_copy(source, target, send, recv, k, q):
-        return pltpu.make_async_remote_copy(
-            src_ref=source.at[k, pl.ds(q, 1)], dst_ref=target.at[k, pl.ds(p, 1)],
-            send_sem=send.at[k, q], recv_sem=recv.at[k, p], device_id=(y, x * n_p + q), device_id_type=MESH,
-        )
-
-    def spread(source, target, send, recv, k):
-        rows = pl.ds(p, 1)
-        pltpu.make_async_copy(source.at[k, rows], target.at[k, rows], recv.at[k, p]).start()
-
-        def one(i, carry):
-            row_copy(source, target, send, recv, k, (p + i) % n_p).start()
-            return carry
-
-        lax.fori_loop(1, n_p, one, 0)
-
-    def collect(target, recv, k):
-        def one(q, carry):
-            rows = target.at[k, pl.ds(q, 1)]
-            pltpu.make_async_copy(rows, rows, recv.at[k, q]).wait()
-            return carry
-
-        lax.fori_loop(0, n_p, one, 0)
-
-    def settle(source, target, send, recv, k):
-        def one(i, carry):
-            row_copy(source, target, send, recv, k, (p + i) % n_p).wait_send()
-            return carry
-
-        lax.fori_loop(1, n_p, one, 0)
-
-    def f1_copy(k, g):
-        return pltpu.make_async_remote_copy(
-            src_ref=sorted_w.at[g, k], dst_ref=f1_in.at[y, k], send_sem=f1_send.at[k, g], recv_sem=f1_recv.at[k, y],
-            device_id=(x, g * n_p + p), device_id_type=MESH,
-        )
-
-    for k in range(stripe):
-        for i in range(n_rep):
-            g = (x + 1 + i) % n_rep
-            stays = diagonal & (g == x)
-
-            @pl.when(stays)
-            def _():
-                pltpu.make_async_copy(sorted_w.at[g, k], f1_in.at[y, k], f1_recv.at[k, y]).start()
-
-            @pl.when(jnp.logical_not(stays))
-            def _():
-                f1_copy(k, g).start()
-
+    for i in range(len(jumps)):
+        pl.semaphore_wait(far_sem.at[i], 1)
+    pl.semaphore_signal(near_sem, inc=1, device_id=(y, partner), device_id_type=MESH)
+    pl.semaphore_wait(near_sem, 1)
+    for k in range(stripe):
         spread(a_out, a_in, a_send, a_recv, k)
 
     def spot(plane):
@@ -302,7 +318,7 @@
             jax.ShapeDtypeStruct(rows.shape, jnp.float32),
             jax.ShapeDtypeStruct(momentum.shape, jnp.float32),
         ),
-        in_specs=[pl.BlockSpec(memory_space=pl.ANY)] * 4,
+        in_specs=[pl.BlockSpec(memory_space=pltpu.HBM)] * 4,
         out_specs=(pl.BlockSpec(memory_space=pl.ANY),) * 2,
         scratch_shapes=[
             vmem((1, blocks), jnp.int32),
@@ -332,6 +348,8 @@
             dma((stripe, n_rep)),
             dma((stripe, n_rep)),
             dma((stripe, n_rep)),
+            pltpu.SemaphoreType.REGULAR((2,)),
+            pltpu.SemaphoreType.REGULAR,
         ],
         compiler_params=pltpu.CompilerParams(collective_id=0, has_side_effects=True, vmem_limit_bytes=64000000),
     )(owners.reshape(1, blocks), rows, anchor, momentum)

time: 63.7 us -> 60.8 us (0.954)
  the two profiles are of different devices: /device:TPU:14 before, /device:TPU:16 now
where the time goes in v3:
time: 60.8 us; the launch traced here: 60.6 us
  Pallas kernels  56.3 us (93%)
  local copies, waits for them, and re-layouts  3.68 us (6%)
  between operations  0.65 us (1%)
    pallas_call x1, Pallas kernels, local(): pl.pallas_call(functools.partial(kernel, n_rep, n_p, stripe, width, block...  56.3 us
    unnamed x4, local copies, waits for them, and re-layouts  3.68 us

profile of v3, /device:TPU:16, one launch (start us, length us, event | category | flops | bytes accessed | tf_op | source)
XLA Modules:
  0.0 60.6 jit_solution(720630289155593102)
XLA Ops:
  0.6 56.3 %shard_map.59 = (f32[3,192,768]{2,1,0:T(8,128)}, f32[2,96,768]{2,1,0:T(8,128)}) custom-call(s32[1,192]{1,0:T(1,128)} %bitcast.7, bf16[3,192,768]{2,1,0:T(8,128)(2,1)} %bitcast.6, f32[2,96,768]{2,1,0:T(8,128)} %a_hbm.1, f32[2,96,768]{2,1,0:T(8,128)} %m_hbm.1), custom_call_target="tpu_custom_call" | custom-call | tf_op jit(solution)/shard_map/pallas_call | solution.py:315
  56.9 0.0 copy-start
  57.0 2.9 %copy.8 = f32[192,3,768]{2,0,1:T(8,128)} copy(f32[192,3,768]{2,0,1:T(8,128)} %bitcast.5) | data formatting | bytes 3538944
  59.8 0.0 copy-done
  59.8 0.8 %copy.9 = f32[2,96,768]{2,1,0:T(8,128)} copy(f32[2,96,768]{2,1,0:T(8,128)S(1)} %copy-done) | data formatting | bytes 1179648
Async XLA Ops:
  56.9 2.9 %copy-start = (f32[2,96,768]{2,1,0:T(8,128)S(1)}, f32[2,96,768]{2,1,0:T(8,128)}, u32[]{:S(2)}) copy-start(f32[2,96,768]{2,1,0:T(8,128)} %get-tuple-element.9) | copy-start | bytes 1769476
